TPU v7x, 32 devices: a whole 2x2x4 slice. The times are simulated.
32 devices in a mesh: dp: 8 (over z, y), table: 4 (over x, core).
Axes of the slice: x: 2, y: 2, z: 4, core: 2. Of those that a mesh axis runs over, the one named last changes fastest.
Arguments:
- expr: bfloat16 [64, 128, 768], P(('dp', 'table')), may hold values from -6 to 6
- gene_owner: int32 [64, 128, 1], P(('dp', 'table')), may hold values from 0 to 7; in each aligned block of 1024 rows (0 to 1023, 1024 to 2047, ..., all dimensions but the last counted through in order) at most 192 rows name the same one
- gene_row: int32 [64, 128], P(('dp', 'table')), may hold values from 0 to 4607
- lengths: int32 [64], P(('dp', 'table')), may hold values from 1 to 128, 6144 in all
- cotangent: bfloat16 [64, 128, 768], P(('dp', 'table')), may hold values from -6 to 6
- tables: bfloat16 [4, 36864, 768], P('table', 'dp'), may hold values from -3 to 3
- w_qkv: bfloat16 [768, 2304], P(('dp', 'table')), may hold values from -0.21875 to 0.21875
- w_out: bfloat16 [768, 768], P(('dp', 'table')), may hold values from -0.875 to 0.875
- w_up: bfloat16 [768, 3072], P(('dp', 'table')), may hold values from -0.21875 to 0.21875
- w_down: bfloat16 [3072, 768], P(('dp', 'table')), may hold values from -0.109375 to 0.109375
- gains: bfloat16 [2, 768], P(None, ('dp', 'table')), may hold values from 0.5 to 1.5
- biases: bfloat16 [6, 768], P(None, ('dp', 'table')), may hold values from -2 to 2
- up_bias: bfloat16 [3072], P(('dp', 'table')), may hold values from -2 to 2
Outputs:
- out: bfloat16 [64, 128, 768], P(('dp', 'table'))
- grad_expr: float32 [64, 128, 768], P(('dp', 'table'))
- grad_tables: float32 [4, 36864, 768], P('table', 'dp')
- grad_w_qkv: float32 [768, 2304], P(('dp', 'table'))
- grad_w_out: float32 [768, 768], P(('dp', 'table'))
- grad_w_up: float32 [768, 3072], P(('dp', 'table'))
- grad_w_down: float32 [3072, 768], P(('dp', 'table'))
- grad_gains: float32 [2, 768], P(None, ('dp', 'table'))
- grad_biases: float32 [6, 768], P(None, ('dp', 'table'))
- grad_up_bias: float32 [3072], P(('dp', 'table'))
Inputs may be any that keep to these rules, and one draw needn't show every extreme that they name: `gene_owner`: in each aligned block of 1024 positions (the slots of the devices that share a dp index), no owner is named more than 192 times, a bound that some block reaches. `lengths`: some slot has length 128.
All inputs are finite; a program needn't handle non-finite values. No bound on the sum of `lengths` on one device may be relied on, other than what follows from the above.
Results may differ from a plain program's by a relative error of at most 0.039.
Values may be sent and summed in bfloat16 or wider, within the bound.
A program may use at most 192 MiB of HBM per device.

v0:
```python
import jax
import jax.numpy as jnp
from jax import lax
from jax.sharding import PartitionSpec as P

HEAD_DIM = 64


def layer_norm(values, scale, shift):
    center = values - jnp.mean(values, axis=-1, keepdims=True)
    spread = jnp.mean(center * center, axis=-1, keepdims=True)
    return center * lax.rsqrt(spread + 1e-05) * scale + shift


def gelu_exact(values):
    return jax.nn.gelu(values, approximate=False)


def fetch(shards):
    return (
        lax.all_gather(shards[0], ("dp", "table"), axis=0, tiled=True),
        lax.all_gather(shards[1], ("dp", "table"), axis=0, tiled=True),
        lax.all_gather(shards[2], ("dp", "table"), axis=0, tiled=True),
        lax.all_gather(shards[3], ("dp", "table"), axis=0, tiled=True),
        lax.all_gather(shards[4], ("dp", "table"), axis=1, tiled=True),
        lax.all_gather(shards[5], ("dp", "table"), axis=1, tiled=True),
        lax.all_gather(shards[6], ("dp", "table"), axis=0, tiled=True),
    )


def attend_scores(queries, key_rows, key_mask):
    scores = (
        jnp.einsum("sqhd,skhd->shqk", queries, key_rows, preferred_element_type=jnp.float32) * 0.125
    )
    return jnp.where(key_mask[:, None, None, :], scores, -1e30)


def micro_pass(weights, hidden_part, cot_part, length_part):
    w_qkv, w_out, w_up, w_down, gain_pair, bias_rows, bias_up = weights
    slots, seq, width = hidden_part.shape
    heads = width // HEAD_DIM
    count = slots * seq
    gain_rows = gain_pair.astype(jnp.float32)
    shift_rows = bias_rows.astype(jnp.float32)
    up_shift = bias_up.astype(jnp.float32)
    qkv_shift = jnp.concatenate([shift_rows[0], jnp.zeros_like(shift_rows[0]), shift_rows[1]])
    key_mask = jnp.arange(seq)[None, :] < length_part[:, None]
    row_keep = key_mask.reshape(count, 1).astype(jnp.float32)
    hidden_in = hidden_part.reshape(count, width)
    hidden_low = hidden_in.astype(jnp.bfloat16)
    projected = jnp.dot(hidden_low, w_qkv, preferred_element_type=jnp.float32) + qkv_shift
    project_low = projected.astype(jnp.bfloat16).reshape(slots, seq, 3, heads, HEAD_DIM)
    queries = project_low[:, :, 0]
    key_rows = project_low[:, :, 1]
    value_rows = project_low[:, :, 2]
    scores = attend_scores(queries, key_rows, key_mask)
    row_max = jnp.max(scores, axis=-1, keepdims=True)
    raised = jnp.exp(scores - row_max)
    row_total = jnp.sum(raised, axis=-1, keepdims=True)
    log_total = row_max + jnp.log(row_total)
    probs_low = (raised / row_total).astype(jnp.bfloat16)
    mixed = jnp.einsum("shqk,skhd->sqhd", probs_low, value_rows, preferred_element_type=jnp.float32)
    mixed_low = mixed.reshape(count, width).astype(jnp.bfloat16)
    branch = jnp.dot(mixed_low, w_out, preferred_element_type=jnp.float32) + shift_rows[2]
    normed, first_back = jax.vjp(layer_norm, hidden_in + branch, gain_rows[0], shift_rows[4])
    normed_low = normed.astype(jnp.bfloat16)
    inner = jnp.dot(normed_low, w_up, preferred_element_type=jnp.float32) + up_shift
    active, gelu_back = jax.vjp(gelu_exact, inner)
    active_low = active.astype(jnp.bfloat16)
    feed = jnp.dot(active_low, w_down, preferred_element_type=jnp.float32) + shift_rows[3]
    final, second_back = jax.vjp(layer_norm, normed + feed, gain_rows[1], shift_rows[5])
    output = (final * row_keep).astype(jnp.bfloat16).reshape(slots, seq, width)
    grad_final = cot_part.reshape(count, width).astype(jnp.float32) * row_keep
    grad_h2, grad_gain_two, grad_shift_two = second_back(grad_final)
    grad_feed = grad_h2.astype(jnp.bfloat16)
    grad_down = jnp.einsum("rf,rd->fd", active_low, grad_feed, preferred_element_type=jnp.float32)
    grad_down_shift = jnp.sum(grad_feed, axis=0, dtype=jnp.float32)
    grad_active = jnp.einsum("rd,fd->rf", grad_feed, w_down, preferred_element_type=jnp.float32)
    grad_inner = gelu_back(grad_active)[0].astype(jnp.bfloat16)
    grad_up = jnp.einsum("rd,rf->df", normed_low, grad_inner, preferred_element_type=jnp.float32)
    grad_up_shift = jnp.sum(grad_inner, axis=0, dtype=jnp.float32)
    grad_normed = grad_h2 + jnp.einsum(
        "rf,df->rd", grad_inner, w_up, preferred_element_type=jnp.float32
    )
    grad_h, grad_gain_one, grad_shift_one = first_back(grad_normed)
    grad_branch = grad_h.astype(jnp.bfloat16)
    grad_out = jnp.einsum("rd,re->de", mixed_low, grad_branch, preferred_element_type=jnp.float32)
    grad_out_shift = jnp.sum(grad_branch, axis=0, dtype=jnp.float32)
    grad_mixed = jnp.einsum("re,de->rd", grad_branch, w_out, preferred_element_type=jnp.float32)
    grad_mixed_low = grad_mixed.astype(jnp.bfloat16).reshape(slots, seq, heads, HEAD_DIM)
    probs_again = jnp.exp(attend_scores(queries, key_rows, key_mask) - log_total)
    grad_probs = jnp.einsum(
        "sqhd,skhd->shqk", grad_mixed_low, value_rows, preferred_element_type=jnp.float32
    )
    row_dot = jnp.sum(probs_again * grad_probs, axis=-1, keepdims=True)
    grad_scores = (probs_again * (grad_probs - row_dot)).astype(jnp.bfloat16)
    grad_queries = (
        jnp.einsum("shqk,skhd->sqhd", grad_scores, key_rows, preferred_element_type=jnp.float32)
        * 0.125
    )
    grad_keys = (
        jnp.einsum("shqk,sqhd->skhd", grad_scores, queries, preferred_element_type=jnp.float32)
        * 0.125
    )
    grad_values = jnp.einsum(
        "shqk,sqhd->skhd",
        probs_again.astype(jnp.bfloat16),
        grad_mixed_low,
        preferred_element_type=jnp.float32,
    )
    grad_project = (
        jnp.stack([grad_queries, grad_keys, grad_values], axis=2)
        .reshape(count, 3 * width)
        .astype(jnp.bfloat16)
    )
    grad_qkv = jnp.einsum("rd,re->de", hidden_low, grad_project, preferred_element_type=jnp.float32)
    project_sums = jnp.sum(grad_project, axis=0, dtype=jnp.float32)
    grad_input = grad_h + jnp.einsum(
        "re,de->rd", grad_project, w_qkv, preferred_element_type=jnp.float32
    )
    grad_gain_pair = jnp.stack([grad_gain_one, grad_gain_two])
    grad_bias_rows = jnp.stack(
        [
            project_sums[:width],
            project_sums[2 * width :],
            grad_out_shift,
            grad_down_shift,
            grad_shift_one,
            grad_shift_two,
        ]
    )
    grads = (grad_qkv, grad_out, grad_up, grad_down, grad_gain_pair, grad_bias_rows, grad_up_shift)
    return (output, grad_input.reshape(slots, seq, width), grads)


def local(
    expr,
    gene_owner,
    gene_row,
    lengths,
    cotangent,
    tables,
    w_qkv,
    w_out,
    w_up,
    w_down,
    gains,
    biases,
    up_bias,
):
    micro, seq, width = expr.shape
    tok_dev = micro * seq
    owners_dp = lax.axis_size("dp")
    capacity = 6 * tok_dev // owners_dp
    rows_dev = tables.shape[1]
    owner_all, row_all = (
        lax.all_gather(gene_owner.reshape(tok_dev), "table", axis=0, tiled=True),
        lax.all_gather(gene_row.reshape(tok_dev), "table", axis=0, tiled=True),
    )
    owner_hits = (owner_all[:, None] == jnp.arange(owners_dp, dtype=jnp.int32)[None, :]).astype(
        jnp.int32
    )
    earlier = jnp.cumsum(owner_hits, axis=0) - owner_hits
    slot_index = jnp.sum(earlier * owner_hits, axis=1)
    send_place = owner_all * capacity + slot_index
    requests = (
        jnp.zeros((owners_dp * capacity,), jnp.int32)
        .at[send_place]
        .set(row_all)
        .reshape(owners_dp, capacity)
    )
    table_rows = tables[0]
    asked_rows = lax.all_to_all(requests, "dp", split_axis=0, concat_axis=0, tiled=True)
    found_rows = jnp.take(table_rows, asked_rows, axis=0)
    returned = lax.all_to_all(found_rows, "dp", split_axis=0, concat_axis=0, tiled=True)
    picked = returned.reshape(owners_dp * capacity, width)[send_place]
    embedded = lax.psum_scatter(
        picked.astype(jnp.float32).astype(jnp.bfloat16), "table", scatter_dimension=0, tiled=True
    ).astype(jnp.float32)
    hidden_all = expr.astype(jnp.float32) + embedded.reshape(micro, seq, width)
    shards = (w_qkv, w_out, w_up, w_down, gains, biases, up_bias)
    totals = None
    outputs = []
    input_grads = []
    for index_micro in range(micro):
        weights = fetch(shards)
        output, grad_input, grads = micro_pass(
            weights,
            hidden_all[index_micro : index_micro + 1],
            cotangent[index_micro : index_micro + 1],
            lengths[index_micro : index_micro + 1],
        )
        outputs.append(output)
        input_grads.append(grad_input)
        totals = (
            grads
            if totals is None
            else jax.tree.map(lambda left, right: left + right, totals, grads)
        )
    out = jnp.concatenate(outputs, axis=0)
    grad_expr = jnp.concatenate(input_grads, axis=0)
    summed = (
        lax.psum_scatter(totals[0], ("dp", "table"), scatter_dimension=0, tiled=True),
        lax.psum_scatter(totals[1], ("dp", "table"), scatter_dimension=0, tiled=True),
        lax.psum_scatter(totals[2], ("dp", "table"), scatter_dimension=0, tiled=True),
        lax.psum_scatter(totals[3], ("dp", "table"), scatter_dimension=0, tiled=True),
        lax.psum_scatter(totals[4], ("dp", "table"), scatter_dimension=1, tiled=True),
        lax.psum_scatter(totals[5], ("dp", "table"), scatter_dimension=1, tiled=True),
        lax.psum_scatter(totals[6], ("dp", "table"), scatter_dimension=0, tiled=True),
    )
    grad_flat = grad_expr.reshape(tok_dev, width)
    grad_group = lax.all_gather(grad_flat.astype(jnp.bfloat16), "table", axis=0, tiled=True).astype(
        grad_flat.dtype
    )
    outgoing = (
        jnp.zeros((owners_dp * capacity, width), jnp.float32)
        .at[send_place]
        .set(grad_group)
        .reshape(owners_dp, capacity, width)
    )
    incoming = lax.all_to_all(
        outgoing.astype(jnp.bfloat16), "dp", split_axis=0, concat_axis=0, tiled=True
    ).astype(outgoing.dtype)
    table_grad = jax.ops.segment_sum(
        incoming.reshape(owners_dp * capacity, width),
        asked_rows.reshape(owners_dp * capacity),
        num_segments=rows_dev,
    )
    return (
        out,
        grad_expr,
        table_grad[None],
        summed[0],
        summed[1],
        summed[2],
        summed[3],
        summed[4],
        summed[5],
        summed[6],
    )


def solution(mesh):
    placed = (
        P(("dp", "table"), None, None),
        P(("dp", "table"), None, None),
        P(("dp", "table"), None),
        P(("dp", "table")),
        P(("dp", "table"), None, None),
        P("table", "dp", None),
        P(("dp", "table"), None),
        P(("dp", "table"), None),
        P(("dp", "table"), None),
        P(("dp", "table"), None),
        P(None, ("dp", "table")),
        P(None, ("dp", "table")),
        P(("dp", "table")),
    )
    return jax.shard_map(
        local,
        mesh=mesh,
        in_specs=placed,
        out_specs=(
            P(("dp", "table"), None, None),
            P(("dp", "table"), None, None),
            P("table", "dp", None),
            P(("dp", "table"), None),
            P(("dp", "table"), None),
            P(("dp", "table"), None),
            P(("dp", "table"), None),
            P(None, ("dp", "table")),
            P(None, ("dp", "table")),
            P(("dp", "table")),
        ),
        check_vma=False,
    )
```

profile of v0, /device:TPU:0, one launch (start us, length us, event | category | flops | bytes accessed | tf_op | source)
XLA Modules:
  0.0 955.6 jit_solution(10269966646609878140)
XLA Ops:
  8.1 6.3 all-gather
  14.3 5.5 all-gather.1
  19.8 2.3 reduce-window.6
  23.2 4.3 scatter_custom_fusion
  27.6 12.4 %all_to_all.25 = s32[8,1,192]{2,1,0:T(1,128)S(1)} all-to-all(s32[8,1,192]{2,1,0:T(1,128)S(1)} %all_to_all.16), channel_id=1, replica_groups=mesh['dp'=8,'table'=4] {'dp'}, dimensions={0} | all-to-all | bytes 12288 | tf_op jit(solution)/shard_map/all_to_all | solution.py:173
  40.1 10.0 %gather_fusion = bf16[1536,768]{1,0:T(8,128)(2,1)S(1)} fusion(bf16[4608,768]{1,0:T(8,128)(2,1)} %bitcast.233, s32[2048]{0:T(1024)S(1)} %pad_clamp_fusion), kind=kCustom, calls=%fused_computation | custom fusion | bytes 4724736 | tf_op jit(solution)/shard_map/jit(_take)/gather | solution.py:174
  50.5 55.8 %all_to_all.26 = bf16[8,192,768]{2,1,0:T(8,128)(2,1)S(1)} all-to-all(bf16[8,192,768]{2,1,0:T(8,128)(2,1)S(1)} %broadcast_select_fusion), channel_id=1, replica_groups=mesh['dp'=8,'table'=4] {'dp'}, dimensions={0} | all-to-all | bytes 4718592 | tf_op jit(solution)/shard_map/all_to_all | solution.py:175
  106.2 5.2 gather_fusion.1
  114.3 39.1 %all-reduce = bf16[3072]{0:T(1024)(128)(2,1)S(1)} all-reduce(bf16[3072]{0:T(1024)(128)(2,1)S(1)} %dynamic-update-slice), channel_id=1, replica_groups=mesh['dp'=8,'table'=4] {'dp','table'}, use_global_device_ids=true, to_apply=%add | all-reduce | flops 3072 | bytes 12288
  154.0 40.3 %all-gather.3 = bf16[32,24,2]{1,2,0:T(2,128)(2,1)S(1)} all-gather(bf16[1,24,2]{1,2,0:T(2,128)(2,1)S(1)} %bitcast.274), channel_id=1, replica_groups=mesh['dp'=8,'table'=4] {'dp','table'}, dimensions={0}, use_global_device_ids=true | all-gather | bytes 3168 | tf_op jit(solution)/shard_map/all_gather | solution.py:25
  194.6 37.2 %all-gather.2 = bf16[32,24,6]{1,2,0:T(8,128)(2,1)S(1)} all-gather(bf16[1,24,6]{1,2,0:T(8,128)(2,1)S(1)} %bitcast.271), channel_id=1, replica_groups=mesh['dp'=8,'table'=4] {'dp','table'}, dimensions={0}, use_global_device_ids=true | all-gather | bytes 9504 | tf_op jit(solution)/shard_map/all_gather | solution.py:26
  238.7 1.9 convert_add_fusion
  240.7 3.7 fusion.4
  244.4 2.1 copy.75
  246.5 2.5 fusion.3
  249.0 2.1 copy.71
  254.0 1.9 convolution_convert_fusion.3
  255.8 1.9 fusion.94
  263.6 32.1 %all-gather.14.cloned.1.call-done = bf16[768,3072]{1,0:T(8,128)(2,1)} async-done(((bf16[24,3072]{1,0:T(8,128)(2,1)}), bf16[768,3072]{1,0:T(8,128)(2,1)}) %all-gather.14.cloned.1.call-update) | async-done | bytes 4718608 | tf_op jit(solution)/shard_map/all_gather | solution.py:23
  295.7 8.5 multiply_convert_fusion
  304.2 57.0 %all-gather.16.cloned.1.call-done = bf16[3072,768]{1,0:T(8,128)(2,1)} async-done(((bf16[96,768]{1,0:T(8,128)(2,1)}), bf16[3072,768]{1,0:T(8,128)(2,1)}) %all-gather.16.cloned.1.call-update) | async-done | bytes 4718608 | tf_op jit(solution)/shard_map/all_gather | solution.py:24
  361.3 3.7 fusion.98
  365.4 5.7 multiply_convert_fusion.1
  376.1 2.4 convert_reduce_fusion
  378.5 1.7 convolution_add_fusion.11
  380.3 2.4 convert_reduce_fusion.1
  382.7 2.4 multiply_reduce_fusion.3
  385.2 1.5 fusion.84
  390.0 1.7 copy.77
  391.8 2.3 convolution_bitcast_fusion.1
  394.1 1.4 multiply_reduce_fusion.1
  400.3 1.7 copy.81
  402.1 1.7 convolution_bitcast_fusion
  403.8 1.4 multiply_reduce_fusion
  413.2 1.9 convolution_add_fusion.7
  417.5 4.0 convolution_add_fusion
  422.8 1.5 fusion.80
  424.3 5.1 convolution_add_fusion.2
  430.7 1.4 fusion.100
  432.1 5.1 convolution_add_fusion.1
  437.3 8.0 scatter_custom_fusion.1
  445.3 4.2 convert_element_type.316
  449.6 3.9 all-to-all-start.2
  454.3 82.2 %all-reduce.4 = (f32[2,768]{1,0:T(2,128)S(1)}, f32[6,768]{1,0:T(8,128)S(1)}, f32[3072]{0:T(1024)S(1)}) all-reduce(f32[2,768]{1,0:T(2,128)S(1)} %maximum_add_fusion, f32[6,768]{1,0:T(8,128)S(1)} %add.291, f32[3072]{0:T(1024)S(1)} %add.292), channel_id=7, replica_groups=mesh['dp'=8,'table'=4] {'dp','table'}, use_global_device_ids=true, to_apply=%region_37.38.clone | all-reduce | flops 9216 | bytes 73728
  539.2 17.2 %scatter_custom_fusion.2 = f32[4608,768]{1,0:T(8,128)} fusion(s32[1536]{0:T(1024)S(1)} %reshape.706, f32[]{:T(128)} %constant.49.clone.1, bf16[1536,768]{1,0:T(8,128)(2,1)S(1)} %bitcast.237), kind=kCustom, calls=%fused_computation.5 | custom fusion | flops 2359296 | bytes 16515076 | tf_op jit(solution)/shard_map/scatter-add | solution.py:224
  556.4 108.2 %reduce-scatter.10.cloned.1.call-done = f32[24,2304]{1,0:T(8,128)} async-done(((f32[768,2304]{1,0:T(8,128)}), f32[24,2304]{1,0:T(8,128)}) %reduce-scatter.10.cloned.1.call-update) | async-done | bytes 221200 | tf_op jit(solution)/shard_map/reduce_scatter | solution.py:203
  664.6 142.2 %reduce-scatter.14.cloned.1.call-done = f32[24,3072]{1,0:T(8,128)} async-done(((f32[768,3072]{1,0:T(8,128)}), f32[24,3072]{1,0:T(8,128)}) %reduce-scatter.14.cloned.1.call-update) | async-done | bytes 294928 | tf_op jit(solution)/shard_map/reduce_scatter | solution.py:205
  806.8 140.9 %reduce-scatter.16.cloned.1.call-done = f32[96,768]{1,0:T(8,128)} async-done(((f32[3072,768]{1,0:T(8,128)}), f32[96,768]{1,0:T(8,128)}) %reduce-scatter.16.cloned.1.call-update) | async-done | bytes 294928 | tf_op jit(solution)/shard_map/reduce_scatter | solution.py:206
  (353 shorter events, 50.0 us)
Async XLA Ops:
  8.0 230.7 %reduce-scatter.8.cloned.1.call-start = ((), (), s32[]{:S(2)}) async-start(), calls=%async_computation.8 | async-start | bytes 1966080 | tf_op jit(solution)/shard_map/reduce_scatter | solution.py:177
  40.0 10.1 %copy-start.54 = (s32[8,1,192]{2,1,0:T(1,128)}, s32[8,1,192]{2,1,0:T(1,128)S(1)}, u32[]{:S(2)}) copy-start(s32[8,1,192]{2,1,0:T(1,128)S(1)} %all_to_all.25) | copy-start | bytes 18436
  111.5 42.5 %copy-start.103 = (bf16[2,24]{1,0:T(2,128)(2,1)S(1)}, bf16[2,24]{1,0:T(2,128)(2,1)}, u32[]{:S(2)}) copy-start(bf16[2,24]{1,0:T(2,128)(2,1)} %param.23) | copy-start | bytes 292
  111.5 83.1 %copy-start.92 = (bf16[6,24]{1,0:T(8,128)(2,1)S(1)}, bf16[6,24]{1,0:T(8,128)(2,1)}, u32[]{:S(2)}) copy-start(bf16[6,24]{1,0:T(8,128)(2,1)} %param.24) | copy-start | bytes 868
  111.5 120.7 %copy-start.93 = (s32[2]{0:T(128)S(1)}, s32[2]{0:T(128)}, u32[]{:S(2)}) copy-start(s32[2]{0:T(128)} %param.16) | copy-start | bytes 28
  111.5 127.3 %copy-start.52 = (bf16[2,128,768]{2,1,0:T(8,128)(2,1)S(1)}, bf16[2,128,768]{2,1,0:T(8,128)(2,1)}, u32[]{:S(2)}) copy-start(bf16[2,128,768]{2,1,0:T(8,128)(2,1)} %param.13) | copy-start | bytes 1179652
  111.5 129.2 %all-gather.10.cloned.1.call-start = ((), (), s32[]{:S(2)}) async-start(), calls=%async_computation.9 | async-start | bytes 3649536 | tf_op jit(solution)/shard_map/all_gather | solution.py:21
  112.1 143.8 %all-gather.12.cloned.1.call-start = ((), (), s32[]{:S(2)}) async-start(), calls=%async_computation.10 | async-start | bytes 1216512 | tf_op jit(solution)/shard_map/all_gather | solution.py:22
  112.7 183.0 %all-gather.14.cloned.1.call-start = ((), (), s32[]{:S(2)}) async-start(), calls=%async_computation.11 | async-start | bytes 4866048 | tf_op jit(solution)/shard_map/all_gather | solution.py:23
  113.3 248.0 %all-gather.16.cloned.1.call-start = ((), (), s32[]{:S(2)}) async-start(), calls=%async_computation.12 | async-start | bytes 4866048 | tf_op jit(solution)/shard_map/all_gather | solution.py:24
  114.0 323.3 %all-gather.18.cloned.1.call-start = ((), (), s32[]{:S(2)}) async-start(), calls=%async_computation.13 | async-start | bytes 1966080 | tf_op jit(solution)/shard_map/all_gather | solution.py:212
  240.7 5.8 copy-start
  258.4 3.5 copy-start.98
  259.6 3.4 copy-start.63
  361.3 4.1 copy-start.1
  361.3 9.8 %slice-start = ((s8[4718592]{0:T(1024)(128)(4,1)}), s8[4194304]{0:T(1024)(128)(4,1)S(1)}, s32[]{:S(2)}) async-start(s8[4718592]{0:T(1024)(128)(4,1)} %bitcast.234), calls=%async_computation.18 | async-start | bytes 8388608
  365.4 5.7 slice-start.1
  365.4 5.8 copy-start.6
  365.4 5.8 copy-start.59
  365.4 5.8 copy-start.65
  365.4 5.8 copy-start.83
  375.4 4.8 copy-start.50
  385.1 3.7 copy-start.3
  391.8 3.7 copy-start.53
  412.2 144.2 %reduce-scatter.12.cloned.1.call-start = ((), (), s32[]{:S(2)}) async-start(), calls=%async_computation.15 | async-start | bytes 2433024 | tf_op jit(solution)/shard_map/reduce_scatter | solution.py:204
  415.1 249.5 %reduce-scatter.10.cloned.1.call-start = ((), (), s32[]{:S(2)}) async-start(), calls=%async_computation.14 | async-start | bytes 7299072 | tf_op jit(solution)/shard_map/reduce_scatter | solution.py:203
  421.6 385.2 %reduce-scatter.14.cloned.1.call-start = ((), (), s32[]{:S(2)}) async-start(), calls=%async_computation.16 | async-start | bytes 9732096 | tf_op jit(solution)/shard_map/reduce_scatter | solution.py:205
  429.5 518.2 %reduce-scatter.16.cloned.1.call-start = ((), (), s32[]{:S(2)}) async-start(), calls=%async_computation.17 | async-start | bytes 9732096 | tf_op jit(solution)/shard_map/reduce_scatter | solution.py:206
  449.5 4.0 copy-start.55
  449.5 4.1 copy-start.70
  449.5 4.1 copy-start.69
  449.5 4.2 copy-start.68
  449.5 4.2 copy-start.67
  449.5 4.2 copy-start.71
  449.5 4.2 copy-start.72
  449.5 4.2 copy-start.76
  449.5 4.2 copy-start.75
  449.5 4.2 copy-start.74
  449.5 4.2 copy-start.73
  449.6 4.3 copy-start.78
  449.6 4.3 copy-start.77
  449.6 4.3 copy-start.57
  449.6 4.5 copy-start.56
  449.6 4.6 copy-start.85
  449.6 4.6 copy-start.86
  449.6 88.8 %copy-start.45 = (bf16[1,128,768]{2,1,0:T(8,128)(2,1)S(1)}, bf16[1,128,768]{2,1,0:T(8,128)(2,1)}, u32[]{:S(2)}) copy-start(bf16[1,128,768]{2,1,0:T(8,128)(2,1)} %get-tuple-element.68) | copy-start | bytes 589828
  449.6 88.8 %copy-start.46 = (bf16[1,128,768]{2,1,0:T(8,128)(2,1)S(1)}, bf16[1,128,768]{2,1,0:T(8,128)(2,1)}, u32[]{:S(2)}) copy-start(bf16[1,128,768]{2,1,0:T(8,128)(2,1)} %get-tuple-element.69) | copy-start | bytes 589828
  449.6 89.6 %all-to-all-start.2 = ((bf16[8,192,768]{2,1,0:T(8,128)(2,1)}), bf16[8,192,768]{2,1,0:T(8,128)(2,1)S(1)}, u32[]{:S(2)}, u32[]{:S(2)}) async-start(bf16[8,192,768]{2,1,0:T(8,128)(2,1)} %bitcast.239), calls=%async_computation.3 | async-start | bytes 4718592 | tf_op jit(solution)/shard_map/all_to_all | solution.py:221
  (72 other events, 121.8 us)
Sparse Core Ops, SparseCore 0:
  111.6 27.1 reduce-scatter.7
  412.3 17.8 all-gather.17
Sparse Core Ops, SparseCore 1:
  114.9 59.5 all-gather.9
  177.3 52.7 all-gather.11
  232.8 62.8 all-gather.13
  299.1 62.1 all-gather.15
  419.7 120.9 reduce-scatter.11
  546.9 117.7 reduce-scatter.9
  672.0 134.8 reduce-scatter.13
  813.1 134.5 reduce-scatter.15
where the time goes:
time: 962 us; the launch traced here: 956 us
  waiting for transfers between devices  483 us (50%)
  blocking collectives  279 us (29%)
  matrix products  75.1 us (8%)
  other arithmetic  53.3 us (6%)
  local copies, waits for them, and re-layouts  43.6 us (5%)
  between operations  17.4 us (2%)
    reduce_scatter x1, waiting for transfers between devices, local(): lax.psum_scatter(totals[2], ('dp', 'table'), scatter_dimension=0, tiled=T...  142 us
    reduce_scatter x1, waiting for transfers between devices, local(): lax.psum_scatter(totals[3], ('dp', 'table'), scatter_dimension=0, tiled=T...  141 us
    unnamed x2, blocking collectives  121 us
    reduce_scatter x1, waiting for transfers between devices, local(): lax.psum_scatter(totals[0], ('dp', 'table'), scatter_dimension=0, tiled=T...  108 us
    all_gather x1, waiting for transfers between devices, fetch(): lax.all_gather(shards[3], ('dp', 'table'), axis=0, tiled=True)  57 us
    all_to_all x1, blocking collectives, local(): lax.all_to_all(found_rows, 'dp', split_axis=0, concat_axis=0, tiled=True)  55.8 us
    all_gather x1, blocking collectives, fetch(): lax.all_gather(shards[4], ('dp', 'table'), axis=1, tiled=True)  40.3 us
    all_gather x1, blocking collectives, fetch(): lax.all_gather(shards[5], ('dp', 'table'), axis=1, tiled=True)  37.2 us
  transfers between devices with their start and end apart: 11, of which 5 were waited for; matrix products, arithmetic and copies ran while one was open for 9% of the time, Pallas kernels for 0%

commit v1 on v0

v1 whole, which is shorter than its diff:
```python
import jax
import jax.numpy as jnp
from jax import lax
from jax.sharding import PartitionSpec as P

HEAD_DIM = 64
AXES = ("dp", "table")


def layer_norm(values, scale, shift):
    center = values - jnp.mean(values, axis=-1, keepdims=True)
    spread = jnp.mean(center * center, axis=-1, keepdims=True)
    return center * lax.rsqrt(spread + 1e-05) * scale + shift


def gelu_exact(values):
    return jax.nn.gelu(values, approximate=False)


class Grid:
    def __init__(self):
        dp, table = lax.axis_size("dp"), lax.axis_size("table")
        self.count = dp * table
        self.high = dp // 2
        self.side = table // 2
        self.bit_core = 1
        self.bit_x = 2
        self.bit_y = table
        self.bit_z = 2 * table
        me_dp, me_table = lax.axis_index("dp"), lax.axis_index("table")
        self.z, self.y = me_dp // 2, me_dp % 2
        self.x, self.core = me_table // 2, me_table % 2

    def swap(self, value, mask):
        pairs = [(index, index ^ mask) for index in range(self.count)]
        return lax.ppermute(value, AXES, pairs)


def ordered(flag, own, other, axis):
    first = flag == 0
    return jnp.stack([jnp.where(first, own, other), jnp.where(first, other, own)], axis=axis)


def pick(values, index, axis):
    return lax.dynamic_index_in_dim(values, index, axis=axis, keepdims=False)


def gather_chunk(grid, shard, x_first):
    rows = [shard] + [grid.swap(shard, grid.bit_z * step) for step in range(1, grid.high)]
    line = jnp.stack(rows)
    place = jnp.arange(grid.high) ^ grid.z
    line = jnp.stack(
        [
            sum_select([(place[spot] == step, rows[step]) for step in range(grid.high)])
            for spot in range(grid.high)
        ]
    )
    first, second = (grid.bit_x, grid.bit_y) if x_first else (grid.bit_y, grid.bit_x)
    one = grid.swap(line, first)
    two = grid.swap(line, second)
    three = grid.swap(one, second)
    if x_first:
        own_y, other_y = ordered(grid.x, line, one, 1), ordered(grid.x, two, three, 1)
        plane = ordered(grid.y, own_y, other_y, 1)
    else:
        own_x, other_x = ordered(grid.y, line, one, 1), ordered(grid.y, two, three, 1)
        plane = ordered(grid.x, own_x, other_x, 2)
    partner = grid.swap(plane, grid.bit_core)
    whole = ordered(grid.core, plane, partner, 3)
    return whole.reshape((grid.count,) + shard.shape)


def sum_select(choices):
    result = choices[-1][1]
    for test, value in choices[:-1]:
        result = jnp.where(test, value, result)
    return result


def scatter_chunk(grid, grads, x_first):
    rows = grads.shape[0] // grid.count
    blocks = grads.reshape((grid.high, 2, grid.side, 2, rows, grads.shape[1]))
    low = jnp.bfloat16

    def halve(value, flag, axis, bit):
        sent = grid.swap(pick(value, 1 - flag, axis).astype(low), bit)
        return pick(value, flag, axis).astype(jnp.float32) + sent.astype(jnp.float32)

    part = halve(blocks, grid.core, 3, grid.bit_core).astype(low)
    if x_first:
        part = halve(part, grid.x, 2, grid.bit_x).astype(low)
        part = halve(part, grid.y, 1, grid.bit_y).astype(low)
    else:
        part = halve(part, grid.y, 1, grid.bit_y).astype(low)
        part = halve(part, grid.x, 1, grid.bit_x).astype(low)
    total = pick(part, grid.z, 0).astype(jnp.float32)
    for step in range(1, grid.high):
        total = total + grid.swap(pick(part, grid.z ^ step, 0), grid.bit_z * step).astype(jnp.float32)
    return total


def attend_scores(queries, key_rows, key_mask):
    scores = (
        jnp.einsum("sqhd,skhd->shqk", queries, key_rows, preferred_element_type=jnp.float32) * 0.125
    )
    return jnp.where(key_mask[:, None, None, :], scores, -1e30)


def layer_pass(weights, hidden_part, cot_part, length_part):
    w_qkv, w_out, w_up, w_down, gain_rows, shift_rows, up_shift = weights
    slots, seq, width = hidden_part.shape
    heads = width // HEAD_DIM
    count = slots * seq
    qkv_shift = jnp.concatenate([shift_rows[0], jnp.zeros_like(shift_rows[0]), shift_rows[1]])
    key_mask = jnp.arange(seq)[None, :] < length_part[:, None]
    row_keep = key_mask.reshape(count, 1).astype(jnp.float32)
    hidden_in = hidden_part.reshape(count, width)
    hidden_low = hidden_in.astype(jnp.bfloat16)
    projected = jnp.dot(hidden_low, w_qkv, preferred_element_type=jnp.float32) + qkv_shift
    project_low = projected.astype(jnp.bfloat16).reshape(slots, seq, 3, heads, HEAD_DIM)
    queries = project_low[:, :, 0]
    key_rows = project_low[:, :, 1]
    value_rows = project_low[:, :, 2]
    scores = attend_scores(queries, key_rows, key_mask)
    row_max = jnp.max(scores, axis=-1, keepdims=True)
    raised = jnp.exp(scores - row_max)
    row_total = jnp.sum(raised, axis=-1, keepdims=True)
    probs = raised / row_total
    probs_low = probs.astype(jnp.bfloat16)
    mixed = jnp.einsum("shqk,skhd->sqhd", probs_low, value_rows, preferred_element_type=jnp.float32)
    mixed_low = mixed.reshape(count, width).astype(jnp.bfloat16)
    branch = jnp.dot(mixed_low, w_out, preferred_element_type=jnp.float32) + shift_rows[2]
    normed, first_back = jax.vjp(layer_norm, hidden_in + branch, gain_rows[0], shift_rows[4])
    normed_low = normed.astype(jnp.bfloat16)
    inner = jnp.dot(normed_low, w_up, preferred_element_type=jnp.float32) + up_shift
    active, gelu_back = jax.vjp(gelu_exact, inner)
    active_low = active.astype(jnp.bfloat16)
    feed = jnp.dot(active_low, w_down, preferred_element_type=jnp.float32) + shift_rows[3]
    final, second_back = jax.vjp(layer_norm, normed + feed, gain_rows[1], shift_rows[5])
    output = (final * row_keep).astype(jnp.bfloat16).reshape(slots, seq, width)
    grad_final = cot_part.reshape(count, width).astype(jnp.float32) * row_keep
    grad_h2, grad_gain_two, grad_shift_two = second_back(grad_final)
    grad_feed = grad_h2.astype(jnp.bfloat16)
    grad_down = jnp.einsum("rf,rd->fd", active_low, grad_feed, preferred_element_type=jnp.float32)
    grad_down_shift = jnp.sum(grad_feed, axis=0, dtype=jnp.float32)
    grad_active = jnp.einsum("rd,fd->rf", grad_feed, w_down, preferred_element_type=jnp.float32)
    grad_inner = gelu_back(grad_active)[0].astype(jnp.bfloat16)
    grad_up = jnp.einsum("rd,rf->df", normed_low, grad_inner, preferred_element_type=jnp.float32)
    grad_up_shift = jnp.sum(grad_inner, axis=0, dtype=jnp.float32)
    grad_normed = grad_h2 + jnp.einsum(
        "rf,df->rd", grad_inner, w_up, preferred_element_type=jnp.float32
    )
    grad_h, grad_gain_one, grad_shift_one = first_back(grad_normed)
    grad_branch = grad_h.astype(jnp.bfloat16)
    grad_out = jnp.einsum("rd,re->de", mixed_low, grad_branch, preferred_element_type=jnp.float32)
    grad_out_shift = jnp.sum(grad_branch, axis=0, dtype=jnp.float32)
    grad_mixed = jnp.einsum("re,de->rd", grad_branch, w_out, preferred_element_type=jnp.float32)
    grad_mixed_low = grad_mixed.astype(jnp.bfloat16).reshape(slots, seq, heads, HEAD_DIM)
    grad_probs = jnp.einsum(
        "sqhd,skhd->shqk", grad_mixed_low, value_rows, preferred_element_type=jnp.float32
    )
    row_dot = jnp.sum(probs * grad_probs, axis=-1, keepdims=True)
    grad_scores = (probs * (grad_probs - row_dot)).astype(jnp.bfloat16)
    grad_queries = (
        jnp.einsum("shqk,skhd->sqhd", grad_scores, key_rows, preferred_element_type=jnp.float32)
        * 0.125
    )
    grad_keys = (
        jnp.einsum("shqk,sqhd->skhd", grad_scores, queries, preferred_element_type=jnp.float32)
        * 0.125
    )
    grad_values = jnp.einsum(
        "shqk,sqhd->skhd", probs_low, grad_mixed_low, preferred_element_type=jnp.float32
    )
    grad_project = jnp.concatenate(
        [
            grad_queries.reshape(count, width).astype(jnp.bfloat16),
            grad_keys.reshape(count, width).astype(jnp.bfloat16),
            grad_values.reshape(count, width).astype(jnp.bfloat16),
        ],
        axis=1,
    )
    grad_qkv = jnp.einsum("rd,re->de", hidden_low, grad_project, preferred_element_type=jnp.float32)
    project_sums = jnp.sum(grad_project, axis=0, dtype=jnp.float32)
    grad_input = grad_h + jnp.einsum(
        "re,de->rd", grad_project, w_qkv, preferred_element_type=jnp.float32
    )
    small = jnp.stack(
        [
            grad_gain_one,
            grad_gain_two,
            project_sums[:width],
            project_sums[2 * width :],
            grad_out_shift,
            grad_down_shift,
            grad_shift_one,
            grad_shift_two,
        ]
    )
    return (output, grad_input.reshape(slots, seq, width), grad_qkv, grad_out, grad_up, grad_down, small, grad_up_shift)


def one_hot(places, size):
    return (places[:, None] == jnp.arange(size, dtype=jnp.int32)[None, :]).astype(jnp.bfloat16)


def local(
    expr,
    gene_owner,
    gene_row,
    lengths,
    cotangent,
    tables,
    w_qkv,
    w_out,
    w_up,
    w_down,
    gains,
    biases,
    up_bias,
):
    grid = Grid()
    micro, seq, width = expr.shape
    tok = micro * seq
    n_dp, n_table = lax.axis_size("dp"), lax.axis_size("table")
    group = n_table * tok
    capacity = 6 * tok // n_dp
    half = capacity // 2
    rows_dev = tables.shape[1]
    me_dp = lax.axis_index("dp")
    me_table = lax.axis_index("table")
    low = jnp.bfloat16

    part_rows = w_qkv.shape[0]
    up_cols = up_bias.shape[0] // part_rows
    small_cols = 8 + up_cols
    small = jnp.concatenate(
        [gains.T, biases.T, up_bias.reshape(up_cols, part_rows).T], axis=1
    )
    small = jnp.pad(small, ((0, 0), (0, 128 - small_cols)))
    shard_one = jnp.concatenate([w_qkv, w_out, small], axis=1)

    ids = gene_owner.reshape(tok) * rows_dev + gene_row.reshape(tok)
    all_ids = lax.all_gather(ids, AXES, axis=0, tiled=True).reshape(n_dp, group)
    all_owner = all_ids // rows_dev
    all_row = all_ids - all_owner * rows_dev
    mine = all_owner == me_dp
    ranks = jnp.cumsum(mine.astype(jnp.int32), axis=1) - 1
    match = mine[:, None, :] & (ranks[:, None, :] == jnp.arange(capacity, dtype=jnp.int32)[None, :, None])
    asked = jnp.sum(jnp.where(match, all_row[:, None, :], 0), axis=2)

    group_owner = pick(all_owner, me_dp, 0)
    hits = (group_owner[:, None] == jnp.arange(n_dp, dtype=jnp.int32)[None, :]).astype(jnp.int32)
    earlier = jnp.cumsum(hits, axis=0) - hits
    slot_index = jnp.sum(earlier * hits, axis=1)
    in_own = (slot_index // half) == grid.core
    place = jnp.where(in_own, 0, n_dp * half) + group_owner * half + slot_index % half
    place_dev = place.reshape(n_table, tok)

    found = jnp.take(tables[0], asked.reshape(-1), axis=0).reshape(n_dp, 2, half, width)
    sent = grid.swap(pick(found, 1 - grid.core, 1), grid.bit_core)
    pair = (pick(found, grid.core, 1).astype(jnp.float32) + sent.astype(jnp.float32)).astype(low)
    returned = lax.all_to_all(pair, "dp", split_axis=0, concat_axis=0, tiled=True)
    returned_other = grid.swap(returned, grid.bit_core)
    slots_all = jnp.concatenate(
        [returned.reshape(n_dp * half, width), returned_other.reshape(n_dp * half, width)]
    )
    own_place = pick(place_dev, me_table, 0)
    far_place = pick(place_dev, me_table ^ grid.bit_x, 0)
    far = jnp.dot(one_hot(far_place, 2 * n_dp * half), slots_all, preferred_element_type=jnp.float32)
    near = jnp.dot(one_hot(own_place, 2 * n_dp * half), slots_all, preferred_element_type=jnp.float32)
    embedded = near + grid.swap(far.astype(low), grid.bit_x).astype(jnp.float32)
    hidden = expr.astype(jnp.float32) + embedded.reshape(micro, seq, width)

    one = gather_chunk(grid, shard_one, True).reshape(grid.count * part_rows, -1)
    two = gather_chunk(grid, w_up, False).reshape(grid.count * part_rows, -1)
    full_down = gather_chunk(grid, w_down, True).reshape(grid.count * w_down.shape[0], -1)
    wide = w_qkv.shape[1]
    small_all = one[:, wide + width :].astype(jnp.float32)
    gain_rows = small_all[:, :2].T
    bias_rows = small_all[:, 2:8].T
    up_all = (
        small_all[:, 8:small_cols].reshape(grid.count, part_rows, up_cols).transpose(0, 2, 1).reshape(-1)
    )
    weights = (one[:, :wide], one[:, wide : wide + width], two, full_down, gain_rows, bias_rows, up_all)
    out, grad_expr, grad_qkv, grad_out, grad_up, grad_down, grad_small, grad_up_bias = layer_pass(
        weights, hidden, cotangent, lengths
    )

    sum_down = scatter_chunk(grid, grad_down, True)
    sum_up = scatter_chunk(grid, grad_up, False)
    small_cat = jnp.concatenate(
        [
            grad_small.T,
            grad_up_bias.reshape(grid.count, up_cols, part_rows).transpose(0, 2, 1).reshape(-1, up_cols),
        ],
        axis=1,
    )
    small_cat = jnp.pad(small_cat, ((0, 0), (0, 128 - small_cols)))
    sum_one = scatter_chunk(grid, jnp.concatenate([grad_qkv, grad_out, small_cat], axis=1), True)
    sum_small = sum_one[:, wide + width :]

    flat = grad_expr.reshape(tok, width).astype(low)
    flat_x = grid.swap(flat, grid.bit_x)
    flat_c = grid.swap(flat, grid.bit_core)
    flat_xc = grid.swap(flat_x, grid.bit_core)
    group_grads = jnp.concatenate([flat, flat_c, flat_x, flat_xc])
    places = jnp.concatenate([pick(place_dev, me_table ^ step, 0) for step in range(n_table)])
    choose = (jnp.arange(n_dp * half, dtype=jnp.int32)[:, None] == places[None, :]).astype(low)
    outgoing = jnp.dot(choose, group_grads, preferred_element_type=jnp.float32).astype(low)
    incoming = lax.all_to_all(
        outgoing.reshape(n_dp, half, width), "dp", split_axis=0, concat_axis=0, tiled=True
    )
    incoming_other = grid.swap(incoming, grid.bit_core)
    arrived = ordered(grid.core, incoming, incoming_other, 1).reshape(n_dp * capacity, width)
    table_grad = jax.ops.segment_sum(
        arrived.astype(jnp.float32), asked.reshape(-1), num_segments=rows_dev
    )
    return (
        out,
        grad_expr,
        table_grad[None],
        sum_one[:, :wide],
        sum_one[:, wide : wide + width],
        sum_up,
        sum_down,
        sum_small[:, :2].T,
        sum_small[:, 2:8].T,
        sum_small[:, 8:small_cols].T.reshape(-1),
    )


def solution(mesh):
    both = ("dp", "table")
    placed = (
        P(both, None, None),
        P(both, None, None),
        P(both, None),
        P(both),
        P(both, None, None),
        P("table", "dp", None),
        P(both, None),
        P(both, None),
        P(both, None),
        P(both, None),
        P(None, both),
        P(None, both),
        P(both),
    )
    return jax.shard_map(
        local,
        mesh=mesh,
        in_specs=placed,
        out_specs=(
            P(both, None, None),
            P(both, None, None),
            P("table", "dp", None),
            P(both, None),
            P(both, None),
            P(both, None),
            P(both, None),
            P(None, both),
            P(None, both),
            P(both),
        ),
        check_vma=False,
    )
```

time: 962 us -> 458 us (0.48)
  waiting for transfers between devices: 483 us -> 127 us
  blocking collectives: 279 us -> 42.4 us
  starting transfers between devices: 4.54 us -> 68.6 us
  other arithmetic: 53.3 us -> 87.6 us
  matrix products: 75.1 us -> 54.9 us
  local copies, waits for them, and re-layouts: 43.6 us -> 58.9 us
    reduce_scatter x5 -> x0, waiting for transfers between devices: 391 us -> none  [the longest x1 142 us: local(): lax.psum_scatter(totals[2], ('dp', 'table'), scatter_dimension=0, tiled=T...]
    unnamed x2 -> x0, blocking collectives: 121 us -> none
    ppermute x0 -> x46, waiting for transfers between devices: none -> 116 us  [swap(): return lax.ppermute(value, AXES, pairs)]
    all_gather x5 -> x0, waiting for transfers between devices: 89.2 us -> none  [the longest x1 57 us: fetch(): lax.all_gather(shards[3], ('dp', 'table'), axis=0, tiled=True)]
    all_to_all x2 -> x0, blocking collectives: 68.1 us -> none  [the longest x1 55.8 us: local(): lax.all_to_all(found_rows, 'dp', split_axis=0, concat_axis=0, tiled=True)]
    ppermute x0 -> x46, starting transfers between devices: none -> 53.9 us  [swap(): return lax.ppermute(value, AXES, pairs)]
    all_gather x4 -> x1, blocking collectives: 89.3 us -> 42.4 us  [local(): all_ids = lax.all_gather(ids, AXES, axis=0, tiled=True).reshape(n_dp, group)]
    another operation x2 -> x27, other arithmetic: 2.41 us -> 34.6 us  [the longest x16 26.6 us: ordered(): jnp.stack([jnp.where(first, own, other), jnp.where(first, other, own)], a...]
  transfers between devices with their start and end apart: 11 -> 48, of which waited for: 5 -> 21; matrix products, arithmetic and copies ran while one was open for 9% -> 27% of each run, Pallas kernels for 0% -> 0%
where the time goes in v1:
time: 458 us; the launch traced here: 450 us
  waiting for transfers between devices  127 us (28%)
  other arithmetic  87.6 us (19%)
  starting transfers between devices  68.6 us (15%)
  local copies, waits for them, and re-layouts  58.9 us (13%)
  matrix products  54.9 us (12%)
  blocking collectives  42.4 us (9%)
  between operations  10.6 us (2%)
    ppermute x46, waiting for transfers between devices, swap(): return lax.ppermute(value, AXES, pairs)  116 us
    ppermute x46, starting transfers between devices, swap(): return lax.ppermute(value, AXES, pairs)  53.9 us
    all_gather x1, blocking collectives, local(): all_ids = lax.all_gather(ids, AXES, axis=0, tiled=True).reshape(n_dp, group)  42.4 us
    another operation x16, other arithmetic, ordered(): jnp.stack([jnp.where(first, own, other), jnp.where(first, other, own)], a...  26.6 us
    scatter-add x1, other arithmetic, local(): jax.ops.segment_sum(arrived.astype(jnp.float32), asked.reshape(-1), num_s...  17.7 us
    unnamed x177, local copies, waits for them, and re-layouts  13.8 us
    all_to_all x1, waiting for transfers between devices, local(): lax.all_to_all(outgoing.reshape(n_dp, half, width), 'dp', split_axis=0, c...  10.8 us
    gather x1, local copies, waits for them, and re-layouts, local(): jnp.take(tables[0], asked.reshape(-1), axis=0).reshape(n_dp, 2, half, width)  10 us
  transfers between devices with their start and end apart: 48, of which 21 were waited for; matrix products, arithmetic and copies ran while one was open for 27% of the time, Pallas kernels for 0%

profile of v1, /device:TPU:0, one launch (start us, length us, event | category | flops | bytes accessed | tf_op | source)
XLA Modules:
  0.0 450.1 jit_solution(10070963619618374891)
XLA Ops:
  0.6 3.1 collective-permute-start.11
  3.7 2.6 collective-permute-start.10
  7.2 3.5 collective-permute-start.17
  12.1 42.4 %all-gather = s32[32,1,256]{2,1,0:T(1,128)S(1)} all-gather(s32[1,1,256]{2,1,0:T(1,128)S(1)} %bitcast.409), channel_id=1, replica_groups=mesh['dp'=8,'table'=4] {'dp','table'}, dimensions={0}, use_global_device_ids=true | all-gather | bytes 33792 | tf_op jit(solution)/shard_map/all_gather | solution.py:244
  66.9 10.0 %gather_fusion = bf16[1536,768]{1,0:T(8,128)(2,1)S(1)} fusion(bf16[4608,768]{1,0:T(8,128)(2,1)} %bitcast.358, s32[2048]{0:T(1024)S(1)} %pad_clamp_fusion), kind=kCustom, calls=%fused_computation | custom fusion | bytes 4724736 | tf_op jit(solution)/shard_map/jit(_take)/gather | solution.py:260
  89.2 3.8 collective-permute-start.5
  94.7 3.2 collective-permute-done.19
  101.1 4.7 %collective-permute-done.4 = bf16[24,3200]{1,0:T(8,128)(2,1)S(1)} collective-permute-done((bf16[24,3200]{1,0:T(8,128)(2,1)S(1)}, bf16[24,3200]{1,0:T(8,128)(2,1)S(1)}, u32[]{:S(2)}, u32[]{:S(2)}) %collective-permute-start.4) | collective-permute-done | bytes 153632 | tf_op jit(solution)/shard_map/ppermute | solution.py:36
  105.7 2.7 collective-permute-done.3
  111.2 6.4 %collective-permute-done.13 = bf16[4,24,3072]{2,1,0:T(8,128)(2,1)} collective-permute-done((bf16[4,24,3072]{2,1,0:T(8,128)(2,1)}, bf16[4,24,3072]{2,1,0:T(8,128)(2,1)}, u32[]{:S(2)}, u32[]{:S(2)}) %collective-permute-start.13) | collective-permute-done | bytes 589856 | tf_op jit(solution)/shard_map/ppermute | solution.py:36
  119.6 6.2 %collective-permute-done.20 = bf16[4,96,768]{2,1,0:T(8,128)(2,1)} collective-permute-done((bf16[4,96,768]{2,1,0:T(8,128)(2,1)}, bf16[4,96,768]{2,1,0:T(8,128)(2,1)}, u32[]{:S(2)}, u32[]{:S(2)}) %collective-permute-start.20) | collective-permute-done | bytes 589856 | tf_op jit(solution)/shard_map/ppermute | solution.py:36
  126.9 11.0 %collective-permute-done.6 = bf16[4,24,3200]{2,1,0:T(8,128)(2,1)S(1)} collective-permute-done((bf16[4,24,3200]{2,1,0:T(8,128)(2,1)}, bf16[4,24,3200]{2,1,0:T(8,128)(2,1)S(1)}, u32[]{:S(2)}, u32[]{:S(2)}) %collective-permute-start.6) | collective-permute-done | bytes 614432 | tf_op jit(solution)/shard_map/ppermute | solution.py:36
  141.4 6.5 %all-to-all-start = ((bf16[8,96,768]{2,1,0:T(8,128)(2,1)}), bf16[8,96,768]{2,1,0:T(8,128)(2,1)}, u32[]{:S(2)}, u32[]{:S(2)}) async-start(bf16[8,96,768]{2,1,0:T(8,128)(2,1)} %fusion.24), calls=%async_computation | async-start | bytes 2359296 | tf_op jit(solution)/shard_map/all_to_all | solution.py:263
  150.0 2.7 collective-permute-done.15
  156.5 7.6 %collective-permute-done.22 = bf16[4,96,768]{2,1,0:T(8,128)(2,1)} collective-permute-done((bf16[4,96,768]{2,1,0:T(8,128)(2,1)}, bf16[4,96,768]{2,1,0:T(8,128)(2,1)}, u32[]{:S(2)}, u32[]{:S(2)}) %collective-permute-start.22) | collective-permute-done | bytes 589856 | tf_op jit(solution)/shard_map/ppermute | solution.py:36
  167.8 12.0 %collective-permute-done.8 = bf16[4,24,3200]{2,1,0:T(8,128)(2,1)S(1)} collective-permute-done((bf16[4,24,3200]{2,1,0:T(8,128)(2,1)}, bf16[4,24,3200]{2,1,0:T(8,128)(2,1)S(1)}, u32[]{:S(2)}, u32[]{:S(2)}) %collective-permute-start.8) | collective-permute-done | bytes 614432 | tf_op jit(solution)/shard_map/ppermute | solution.py:36
  184.2 2.6 select_bitcast_fusion.3
  186.9 2.6 pad_maximum_fusion.2
  191.5 2.6 pad_maximum_fusion.1
  196.9 3.0 fusion.48
  204.8 6.2 %collective-permute-done.2 = bf16[256,768]{1,0:T(8,128)(2,1)S(1)} collective-permute-done((bf16[256,768]{1,0:T(8,128)(2,1)S(1)}, bf16[256,768]{1,0:T(8,128)(2,1)S(1)}, u32[]{:S(2)}, u32[]{:S(2)}) %collective-permute-start.2) | collective-permute-done | bytes 393248 | tf_op jit(solution)/shard_map/ppermute | solution.py:36
  217.5 2.6 fusion.112
  224.8 8.1 %multiply_convert_fusion = (bf16[256,3072]{1,0:T(8,128)(2,1)S(1)}, f32[256,3072]{1,0:T(8,128)S(1)}, f32[256,3072]{1,0:T(8,128)S(1)}) fusion(f32[3072]{0:T(1024)S(1)} %copy-done.54, bf16[768,3072]{1,0:T(8,128)(2,1)S(1)} %bitcast.386, f32[256,768]{1,0:T(8,128)S(1)} %get-tuple-element.168, f32[768]{0:T(1024)S(1)} %get-tuple-element.79, ...), kind=kOutput, calls=%fused_computation.30 | convolution fusion | flops 1260847104 | bytes 13389824 | tf_op jit(solution)/shard_map/dot_general | solution.py:135
  238.0 2.8 convert_reduce_fusion
  245.5 2.5 convolution_convert_fusion.1
  260.8 4.1 fusion.116
  265.0 5.4 %fusion.103 = f32[768,3072]{1,0:T(8,128)} fusion(bf16[256,3072]{1,0:T(8,128)(2,1)S(1)} %copy-done.32, f32[256,768]{1,0:T(8,128)S(1)} %get-tuple-element.168, f32[768]{0:T(1024)S(1)} %get-tuple-element.79, f32[768]{0:T(1024)S(1)} %get-tuple-element.177, f32[256]{0:T(256)S(1)} %copy-done.52, f32[256]{0:T(256)S(1)} %copy-done.44), kind=kOutput, calls=%fused_computation.315 | convolution fusion | flops 1208942592 | bytes 11804672 | tf_op jit(solution)/shard_map/rd,rf->df/dot_general | solution.py:148
  270.4 5.1 %fusion.117 = f32[3072,768]{1,0:T(8,128)} fusion(bf16[256,3072]{1,0:T(8,128)(2,1)S(1)} %get-tuple-element.93, bf16[256,768]{1,0:T(8,128)(2,1)S(1)} %copy-done.21), kind=kOutput, calls=%fused_computation.326 | convolution fusion | flops 1207959552 | bytes 11403264 | tf_op jit(solution)/shard_map/rf,rd->fd/dot_general | solution.py:144
  277.7 4.1 fusion.20
  281.8 4.3 fusion.21
  287.8 3.9 copy-done
  293.3 4.5 %collective-permute-done.24 = bf16[256,768]{1,0:T(8,128)(2,1)S(1)} collective-permute-done((bf16[256,768]{1,0:T(8,128)(2,1)S(1)}, bf16[256,768]{1,0:T(8,128)(2,1)S(1)}, u32[]{:S(2)}, u32[]{:S(2)}) %collective-permute-start.24) | collective-permute-done | bytes 393248 | tf_op jit(solution)/shard_map/ppermute | solution.py:36
  298.1 3.7 fusion.36
  301.8 8.2 %all-to-all-start.1 = ((bf16[8,96,768]{2,1,0:T(8,128)(2,1)}), bf16[8,96,768]{2,1,0:T(8,128)(2,1)}, u32[]{:S(2)}, u32[]{:S(2)}) async-start(bf16[8,96,768]{2,1,0:T(8,128)(2,1)} %bitcast.396), calls=%async_computation.1 | async-start | bytes 2359296 | tf_op jit(solution)/shard_map/all_to_all | solution.py:311
  310.1 3.9 fusion.6
  318.6 3.7 fusion.5
  329.0 10.8 %all-to-all-done.1 = bf16[8,96,768]{2,1,0:T(8,128)(2,1)} async-done(((bf16[8,96,768]{2,1,0:T(8,128)(2,1)}), bf16[8,96,768]{2,1,0:T(8,128)(2,1)}, u32[]{:S(2)}, u32[]{:S(2)}) %all-to-all-start.1) | async-done | bytes 1179680 | tf_op jit(solution)/shard_map/all_to_all | solution.py:311
  339.8 11.6 %collective-permute-done.35 = bf16[4,2,24,3072]{3,2,0,1:T(8,128)(2,1)} collective-permute-done((bf16[4,2,24,3072]{3,2,0,1:T(8,128)(2,1)}, bf16[4,2,24,3072]{3,2,0,1:T(8,128)(2,1)}, u32[]{:S(2)}, u32[]{:S(2)}) %collective-permute-start.35) | collective-permute-done | bytes 1179680 | tf_op jit(solution)/shard_map/ppermute | solution.py:36
  357.7 21.4 %collective-permute-done.29 = bf16[4,2,24,3200]{3,2,1,0:T(8,128)(2,1)} collective-permute-done((bf16[4,2,24,3200]{3,2,1,0:T(8,128)(2,1)}, bf16[4,2,24,3200]{3,2,1,0:T(8,128)(2,1)}, u32[]{:S(2)}, u32[]{:S(2)}) %collective-permute-start.29) | collective-permute-done | bytes 1228832 | tf_op jit(solution)/shard_map/ppermute | solution.py:36
  383.6 2.6 copy.255
  386.2 17.7 %scatter_custom_fusion = f32[4608,768]{1,0:T(8,128)} fusion(s32[1536]{0:T(1024)S(1)} %reshape.807, f32[1536,768]{1,0:T(8,128)} %bitcast.388, f32[]{:T(128)} %constant.281.clone.1), kind=kCustom, calls=%fused_computation.5 | custom fusion | flops 1179648 | bytes 14156288 | tf_op jit(solution)/shard_map/scatter-add | solution.py:316
  407.0 2.6 collective-permute-start.39
  413.6 5.0 %collective-permute-start.45 = (bf16[96,768]{1,0:T(8,128)(2,1)S(1)}, bf16[96,768]{1,0:T(8,128)(2,1)S(1)}, u32[]{:S(2)}, u32[]{:S(2)}) collective-permute-start(bf16[96,768]{1,0:T(8,128)(2,1)S(1)} %get-tuple-element.135), channel_id=1, source_target_pairs={{0,24},{1,25},{2,26},{3,27},{4,28},{5,29},{6,30},{7,31},{8,16},{9,... | collective-permute-start | bytes 442376 | tf_op jit(solution)/shard_map/ppermute | solution.py:36
  418.6 3.9 collective-permute-start.44
  422.5 3.9 collective-permute-done.38
  427.4 5.0 %collective-permute-start.31 = (bf16[24,3200]{1,0:T(8,128)(2,1)S(1)}, bf16[24,3200]{1,0:T(8,128)(2,1)S(1)}, u32[]{:S(2)}, u32[]{:S(2)}) collective-permute-start(bf16[24,3200]{1,0:T(8,128)(2,1)S(1)} %get-tuple-element.127), channel_id=1, source_target_pairs={{0,8},{1,9},{2,10},{3,11},{4,12},{5,13},{6,14},{7,15},{8,0},{9,1},... | collective-permute-start | bytes 460808 | tf_op jit(solution)/shard_map/ppermute | solution.py:36
  432.4 3.0 collective-permute-start.33
  440.3 5.9 %collective-permute-done.32 = bf16[24,3200]{1,0:T(8,128)(2,1)S(1)} collective-permute-done((bf16[24,3200]{1,0:T(8,128)(2,1)S(1)}, bf16[24,3200]{1,0:T(8,128)(2,1)S(1)}, u32[]{:S(2)}, u32[]{:S(2)}) %collective-permute-start.32) | collective-permute-done | bytes 153632 | tf_op jit(solution)/shard_map/ppermute | solution.py:36
  (417 shorter events, 134.0 us)
Async XLA Ops:
  0.6 88.5 %collective-permute-start.11 = (bf16[24,3072]{1,0:T(8,128)(2,1)}, bf16[24,3072]{1,0:T(8,128)(2,1)S(1)}, u32[]{:S(2)}, u32[]{:S(2)}) collective-permute-start(bf16[24,3072]{1,0:T(8,128)(2,1)} %param.21), channel_id=1, source_target_pairs={{0,8},{1,9},{2,10},{3,11},{4,12},{5,13},{6,14},{7,15},{8,0},{9,1},... | collective-permute-start | bytes 442376 | tf_op jit(solution)/shard_map/ppermute | solution.py:36
  3.7 85.5 %collective-permute-start.10 = (bf16[24,3072]{1,0:T(8,128)(2,1)}, bf16[24,3072]{1,0:T(8,128)(2,1)S(1)}, u32[]{:S(2)}, u32[]{:S(2)}) collective-permute-start(bf16[24,3072]{1,0:T(8,128)(2,1)} %param.21), channel_id=1, source_target_pairs={{0,16},{1,17},{2,18},{3,19},{4,20},{5,21},{6,22},{7,23},{8,24},{9,... | collective-permute-start | bytes 442376 | tf_op jit(solution)/shard_map/ppermute | solution.py:36
  6.3 86.7 %collective-permute-start.12 = (bf16[24,3072]{1,0:T(8,128)(2,1)}, bf16[24,3072]{1,0:T(8,128)(2,1)S(1)}, u32[]{:S(2)}, u32[]{:S(2)}) collective-permute-start(bf16[24,3072]{1,0:T(8,128)(2,1)} %param.21), channel_id=1, source_target_pairs={{0,24},{1,25},{2,26},{3,27},{4,28},{5,29},{6,30},{7,31},{8,16},{9,... | collective-permute-start | bytes 442376 | tf_op jit(solution)/shard_map/ppermute | solution.py:36
  6.3 87.7 %collective-permute-start.18 = (bf16[96,768]{1,0:T(8,128)(2,1)}, bf16[96,768]{1,0:T(8,128)(2,1)S(1)}, u32[]{:S(2)}, u32[]{:S(2)}) collective-permute-start(bf16[96,768]{1,0:T(8,128)(2,1)} %param.22), channel_id=1, source_target_pairs={{0,8},{1,9},{2,10},{3,11},{4,12},{5,13},{6,14},{7,15},{8,0},{9,1},... | collective-permute-start | bytes 442376 | tf_op jit(solution)/shard_map/ppermute | solution.py:36
  7.2 87.4 %collective-permute-start.17 = (bf16[96,768]{1,0:T(8,128)(2,1)}, bf16[96,768]{1,0:T(8,128)(2,1)S(1)}, u32[]{:S(2)}, u32[]{:S(2)}) collective-permute-start(bf16[96,768]{1,0:T(8,128)(2,1)} %param.22), channel_id=1, source_target_pairs={{0,16},{1,17},{2,18},{3,19},{4,20},{5,21},{6,22},{7,23},{8,24},{9,... | collective-permute-start | bytes 442376 | tf_op jit(solution)/shard_map/ppermute | solution.py:36
  89.1 8.7 %collective-permute-start.19 = (bf16[96,768]{1,0:T(8,128)(2,1)S(1)}, bf16[96,768]{1,0:T(8,128)(2,1)S(1)}, u32[]{:S(2)}, u32[]{:S(2)}) collective-permute-start(bf16[96,768]{1,0:T(8,128)(2,1)S(1)} %copy-done.41), channel_id=1, source_target_pairs={{0,24},{1,25},{2,26},{3,27},{4,28},{5,29},{6,30},{7,31},{8,16},{9,... | collective-permute-start | bytes 442376 | tf_op jit(solution)/shard_map/ppermute | solution.py:36
  89.2 11.8 %collective-permute-start.5 = (bf16[24,3200]{1,0:T(8,128)(2,1)S(1)}, bf16[24,3200]{1,0:T(8,128)(2,1)S(1)}, u32[]{:S(2)}, u32[]{:S(2)}) collective-permute-start(bf16[24,3200]{1,0:T(8,128)(2,1)S(1)} %pad_maximum_fusion.22), channel_id=1, source_target_pairs={{0,24},{1,25},{2,26},{3,27},{4,28},{5,29},{6,30},{7,31},{8,16},{9,... | collective-permute-start | bytes 460808 | tf_op jit(solution)/shard_map/ppermute | solution.py:36
  93.0 12.7 %collective-permute-start.4 = (bf16[24,3200]{1,0:T(8,128)(2,1)S(1)}, bf16[24,3200]{1,0:T(8,128)(2,1)S(1)}, u32[]{:S(2)}, u32[]{:S(2)}) collective-permute-start(bf16[24,3200]{1,0:T(8,128)(2,1)S(1)} %pad_maximum_fusion.22), channel_id=1, source_target_pairs={{0,8},{1,9},{2,10},{3,11},{4,12},{5,13},{6,14},{7,15},{8,0},{9,1},... | collective-permute-start | bytes 460808 | tf_op jit(solution)/shard_map/ppermute | solution.py:36
  94.0 14.4 %collective-permute-start.3 = (bf16[24,3200]{1,0:T(8,128)(2,1)S(1)}, bf16[24,3200]{1,0:T(8,128)(2,1)S(1)}, u32[]{:S(2)}, u32[]{:S(2)}) collective-permute-start(bf16[24,3200]{1,0:T(8,128)(2,1)S(1)} %pad_maximum_fusion.22), channel_id=1, source_target_pairs={{0,16},{1,17},{2,18},{3,19},{4,20},{5,21},{6,22},{7,23},{8,24},{9,... | collective-permute-start | bytes 460808 | tf_op jit(solution)/shard_map/ppermute | solution.py:36
  94.7 45.0 %collective-permute-start = (bf16[8,96,768]{2,1,0:T(8,128)(2,1)S(1)}, bf16[8,96,768]{2,1,0:T(8,128)(2,1)S(1)}, u32[]{:S(2)}, u32[]{:S(2)}) collective-permute-start(bf16[8,96,768]{2,1,0:T(8,128)(2,1)S(1)} %dynamic-slice_bitcast_fusion.3), channel_id=1, source_target_pairs={{0,1},{1,0},{2,3},{3,2},{4,5},{5,4},{6,7},{7,6},{8,9},{9,8},{10,11... | collective-permute-start | bytes 3538952 | tf_op jit(solution)/shard_map/ppermute | solution.py:36
  97.9 50.0 %collective-permute-start.14 = (bf16[4,24,3072]{2,1,0:T(8,128)(2,1)}, bf16[4,24,3072]{2,1,0:T(8,128)(2,1)}, u32[]{:S(2)}, u32[]{:S(2)}) collective-permute-start(bf16[4,24,3072]{2,1,0:T(8,128)(2,1)} %pad_maximum_fusion.20), channel_id=1, source_target_pairs={{0,2},{1,3},{2,0},{3,1},{4,6},{5,7},{6,4},{7,5},{8,10},{9,11},{10,... | collective-permute-start | bytes 1769480 | tf_op jit(solution)/shard_map/ppermute | solution.py:36
  101.0 16.6 %collective-permute-start.13 = (bf16[4,24,3072]{2,1,0:T(8,128)(2,1)}, bf16[4,24,3072]{2,1,0:T(8,128)(2,1)}, u32[]{:S(2)}, u32[]{:S(2)}) collective-permute-start(bf16[4,24,3072]{2,1,0:T(8,128)(2,1)} %pad_maximum_fusion.20), channel_id=1, source_target_pairs={{0,4},{1,5},{2,6},{3,7},{4,0},{5,1},{6,2},{7,3},{8,12},{9,13},{10,... | collective-permute-start | bytes 1769480 | tf_op jit(solution)/shard_map/ppermute | solution.py:36
  105.7 50.8 %collective-permute-start.21 = (bf16[4,96,768]{2,1,0:T(8,128)(2,1)}, bf16[4,96,768]{2,1,0:T(8,128)(2,1)}, u32[]{:S(2)}, u32[]{:S(2)}) collective-permute-start(bf16[4,96,768]{2,1,0:T(8,128)(2,1)} %pad_maximum_fusion.21), channel_id=1, source_target_pairs={{0,4},{1,5},{2,6},{3,7},{4,0},{5,1},{6,2},{7,3},{8,12},{9,13},{10,... | collective-permute-start | bytes 1769480 | tf_op jit(solution)/shard_map/ppermute | solution.py:36
  108.4 17.3 %collective-permute-start.20 = (bf16[4,96,768]{2,1,0:T(8,128)(2,1)}, bf16[4,96,768]{2,1,0:T(8,128)(2,1)}, u32[]{:S(2)}, u32[]{:S(2)}) collective-permute-start(bf16[4,96,768]{2,1,0:T(8,128)(2,1)} %pad_maximum_fusion.21), channel_id=1, source_target_pairs={{0,2},{1,3},{2,0},{3,1},{4,6},{5,7},{6,4},{7,5},{8,10},{9,11},{10,... | collective-permute-start | bytes 1769480 | tf_op jit(solution)/shard_map/ppermute | solution.py:36
  117.6 20.2 %collective-permute-start.6 = (bf16[4,24,3200]{2,1,0:T(8,128)(2,1)}, bf16[4,24,3200]{2,1,0:T(8,128)(2,1)S(1)}, u32[]{:S(2)}, u32[]{:S(2)}) collective-permute-start(bf16[4,24,3200]{2,1,0:T(8,128)(2,1)} %pad_maximum_fusion.19), channel_id=1, source_target_pairs={{0,2},{1,3},{2,0},{3,1},{4,6},{5,7},{6,4},{7,5},{8,10},{9,11},{10,... | collective-permute-start | bytes 1843208 | tf_op jit(solution)/shard_map/ppermute | solution.py:36
  125.7 42.1 %collective-permute-start.7 = (bf16[4,24,3200]{2,1,0:T(8,128)(2,1)}, bf16[4,24,3200]{2,1,0:T(8,128)(2,1)}, u32[]{:S(2)}, u32[]{:S(2)}) collective-permute-start(bf16[4,24,3200]{2,1,0:T(8,128)(2,1)} %pad_maximum_fusion.19), channel_id=1, source_target_pairs={{0,4},{1,5},{2,6},{3,7},{4,0},{5,1},{6,2},{7,3},{8,12},{9,13},{10,... | collective-permute-start | bytes 1843208 | tf_op jit(solution)/shard_map/ppermute | solution.py:36
  137.9 14.8 %collective-permute-start.15 = (bf16[4,24,3072]{2,1,0:T(8,128)(2,1)}, bf16[4,24,3072]{2,1,0:T(8,128)(2,1)}, u32[]{:S(2)}, u32[]{:S(2)}) collective-permute-start(bf16[4,24,3072]{2,1,0:T(8,128)(2,1)} %collective-permute-done.13), channel_id=1, source_target_pairs={{0,2},{1,3},{2,0},{3,1},{4,6},{5,7},{6,4},{7,5},{8,10},{9,11},{10,... | collective-permute-start | bytes 1769480 | tf_op jit(solution)/shard_map/ppermute | solution.py:36
  139.6 24.5 %collective-permute-start.22 = (bf16[4,96,768]{2,1,0:T(8,128)(2,1)}, bf16[4,96,768]{2,1,0:T(8,128)(2,1)}, u32[]{:S(2)}, u32[]{:S(2)}) collective-permute-start(bf16[4,96,768]{2,1,0:T(8,128)(2,1)} %collective-permute-done.20), channel_id=1, source_target_pairs={{0,4},{1,5},{2,6},{3,7},{4,0},{5,1},{6,2},{7,3},{8,12},{9,13},{10,... | collective-permute-start | bytes 1769480 | tf_op jit(solution)/shard_map/ppermute | solution.py:36
  141.4 42.3 %all-to-all-start = ((bf16[8,96,768]{2,1,0:T(8,128)(2,1)}), bf16[8,96,768]{2,1,0:T(8,128)(2,1)}, u32[]{:S(2)}, u32[]{:S(2)}) async-start(bf16[8,96,768]{2,1,0:T(8,128)(2,1)} %fusion.24), calls=%async_computation | async-start | bytes 2359296 | tf_op jit(solution)/shard_map/all_to_all | solution.py:263
  147.9 31.9 %collective-permute-start.8 = (bf16[4,24,3200]{2,1,0:T(8,128)(2,1)}, bf16[4,24,3200]{2,1,0:T(8,128)(2,1)S(1)}, u32[]{:S(2)}, u32[]{:S(2)}) collective-permute-start(bf16[4,24,3200]{2,1,0:T(8,128)(2,1)} %copy-done.34), channel_id=1, source_target_pairs={{0,4},{1,5},{2,6},{3,7},{4,0},{5,1},{6,2},{7,3},{8,12},{9,13},{10,... | collective-permute-start | bytes 1843208 | tf_op jit(solution)/shard_map/ppermute | solution.py:36
  156.5 33.0 %collective-permute-start.16 = (bf16[4,2,2,24,3072]{4,3,2,1,0:T(8,128)(2,1)}, bf16[4,2,2,24,3072]{4,3,2,1,0:T(8,128)(2,1)}, u32[]{:S(2)}, u32[]{:S(2)}) collective-permute-start(bf16[4,2,2,24,3072]{4,3,2,1,0:T(8,128)(2,1)} %pad_maximum_fusion.5), channel_id=1, source_target_pairs={{0,1},{1,0},{2,3},{3,2},{4,5},{5,4},{6,7},{7,6},{8,9},{9,8},{10,11... | collective-permute-start | bytes 7077896 | tf_op jit(solution)/shard_map/ppermute | solution.py:36
  167.8 16.4 %collective-permute-start.23 = (bf16[4,2,2,96,768]{4,3,2,1,0:T(8,128)(2,1)}, bf16[4,2,2,96,768]{4,3,2,1,0:T(8,128)(2,1)}, u32[]{:S(2)}, u32[]{:S(2)}) collective-permute-start(bf16[4,2,2,96,768]{4,3,2,1,0:T(8,128)(2,1)} %pad_maximum_fusion.6), channel_id=1, source_target_pairs={{0,1},{1,0},{2,3},{3,2},{4,5},{5,4},{6,7},{7,6},{8,9},{9,8},{10,11... | collective-permute-start | bytes 7077896 | tf_op jit(solution)/shard_map/ppermute | solution.py:36
  183.0 11.1 %collective-permute-start.9 = (bf16[4,2,2,24,3200]{4,3,2,1,0:T(8,128)(2,1)}, bf16[4,2,2,24,3200]{4,3,2,1,0:T(8,128)(2,1)}, u32[]{:S(2)}, u32[]{:S(2)}) collective-permute-start(bf16[4,2,2,24,3200]{4,3,2,1,0:T(8,128)(2,1)} %pad_maximum_fusion.3), channel_id=1, source_target_pairs={{0,1},{1,0},{2,3},{3,2},{4,5},{5,4},{6,7},{7,6},{8,9},{9,8},{10,11... | collective-permute-start | bytes 7372808 | tf_op jit(solution)/shard_map/ppermute | solution.py:36
  183.7 13.2 %collective-permute-start.1 = (bf16[8,96,768]{2,1,0:T(8,128)(2,1)}, bf16[8,96,768]{2,1,0:T(8,128)(2,1)S(1)}, u32[]{:S(2)}, u32[]{:S(2)}) collective-permute-start(bf16[8,96,768]{2,1,0:T(8,128)(2,1)} %all-to-all-done), channel_id=1, source_target_pairs={{0,1},{1,0},{2,3},{3,2},{4,5},{5,4},{6,7},{7,6},{8,9},{9,8},{10,11... | collective-permute-start | bytes 3538952 | tf_op jit(solution)/shard_map/ppermute | solution.py:36
  199.9 11.1 %collective-permute-start.2 = (bf16[256,768]{1,0:T(8,128)(2,1)S(1)}, bf16[256,768]{1,0:T(8,128)(2,1)S(1)}, u32[]{:S(2)}, u32[]{:S(2)}) collective-permute-start(bf16[256,768]{1,0:T(8,128)(2,1)S(1)} %fusion.48), channel_id=1, source_target_pairs={{0,2},{1,3},{2,0},{3,1},{4,6},{5,7},{6,4},{7,5},{8,10},{9,11},{10,... | collective-permute-start | bytes 1179656 | tf_op jit(solution)/shard_map/ppermute | solution.py:36
  276.2 16.5 %collective-permute-start.25 = (bf16[256,768]{1,0:T(8,128)(2,1)}, bf16[256,768]{1,0:T(8,128)(2,1)}, u32[]{:S(2)}, u32[]{:S(2)}) collective-permute-start(bf16[256,768]{1,0:T(8,128)(2,1)} %get-tuple-element.175), channel_id=1, source_target_pairs={{0,2},{1,3},{2,0},{3,1},{4,6},{5,7},{6,4},{7,5},{8,10},{9,11},{10,... | collective-permute-start | bytes 1179656 | tf_op jit(solution)/shard_map/ppermute | solution.py:36
  281.8 28.3 %collective-permute-start.34 = (bf16[4,2,2,24,3072]{4,3,0,2,1:T(8,128)(2,1)}, bf16[4,2,2,24,3072]{4,3,0,2,1:T(8,128)(2,1)}, u32[]{:S(2)}, u32[]{:S(2)}) collective-permute-start(bf16[4,2,2,24,3072]{4,3,0,2,1:T(8,128)(2,1)} %fusion.20), channel_id=1, source_target_pairs={{0,1},{1,0},{2,3},{3,2},{4,5},{5,4},{6,7},{7,6},{8,9},{9,8},{10,11... | collective-permute-start | bytes 7077896 | tf_op jit(solution)/shard_map/ppermute | solution.py:36
  286.1 32.5 %collective-permute-start.40 = (bf16[4,2,2,96,768]{4,3,0,1,2:T(8,128)(2,1)}, bf16[4,2,2,96,768]{4,3,0,1,2:T(8,128)(2,1)}, u32[]{:S(2)}, u32[]{:S(2)}) collective-permute-start(bf16[4,2,2,96,768]{4,3,0,1,2:T(8,128)(2,1)} %fusion.21), channel_id=1, source_target_pairs={{0,1},{1,0},{2,3},{3,2},{4,5},{5,4},{6,7},{7,6},{8,9},{9,8},{10,11... | collective-permute-start | bytes 7077896 | tf_op jit(solution)/shard_map/ppermute | solution.py:36
  291.9 32.1 %collective-permute-start.28 = (bf16[4,2,2,24,3200]{4,3,2,1,0:T(8,128)(2,1)S(1)}, bf16[4,2,2,24,3200]{4,3,2,1,0:T(8,128)(2,1)}, u32[]{:S(2)}, u32[]{:S(2)}) collective-permute-start(bf16[4,2,2,24,3200]{4,3,2,1,0:T(8,128)(2,1)S(1)} %fusion.18), channel_id=1, source_target_pairs={{0,1},{1,0},{2,3},{3,2},{4,5},{5,4},{6,7},{7,6},{8,9},{9,8},{10,11... | collective-permute-start | bytes 7372808 | tf_op jit(solution)/shard_map/ppermute | solution.py:36
  292.7 5.2 %collective-permute-start.24 = (bf16[256,768]{1,0:T(8,128)(2,1)S(1)}, bf16[256,768]{1,0:T(8,128)(2,1)S(1)}, u32[]{:S(2)}, u32[]{:S(2)}) collective-permute-start(bf16[256,768]{1,0:T(8,128)(2,1)S(1)} %copy-done.71), channel_id=1, source_target_pairs={{0,1},{1,0},{2,3},{3,2},{4,5},{5,4},{6,7},{7,6},{8,9},{9,8},{10,11... | collective-permute-start | bytes 1179656 | tf_op jit(solution)/shard_map/ppermute | solution.py:36
  292.7 5.5 %collective-permute-start.26 = (bf16[256,768]{1,0:T(8,128)(2,1)}, bf16[256,768]{1,0:T(8,128)(2,1)}, u32[]{:S(2)}, u32[]{:S(2)}) collective-permute-start(bf16[256,768]{1,0:T(8,128)(2,1)} %collective-permute-done.25), channel_id=1, source_target_pairs={{0,1},{1,0},{2,3},{3,2},{4,5},{5,4},{6,7},{7,6},{8,9},{9,8},{10,11... | collective-permute-start | bytes 1179656 | tf_op jit(solution)/shard_map/ppermute | solution.py:36
  301.8 38.0 %all-to-all-start.1 = ((bf16[8,96,768]{2,1,0:T(8,128)(2,1)}), bf16[8,96,768]{2,1,0:T(8,128)(2,1)}, u32[]{:S(2)}, u32[]{:S(2)}) async-start(bf16[8,96,768]{2,1,0:T(8,128)(2,1)} %bitcast.396), calls=%async_computation.1 | async-start | bytes 2359296 | tf_op jit(solution)/shard_map/all_to_all | solution.py:311
  316.6 34.9 %collective-permute-start.35 = (bf16[4,2,24,3072]{3,2,0,1:T(8,128)(2,1)}, bf16[4,2,24,3072]{3,2,0,1:T(8,128)(2,1)}, u32[]{:S(2)}, u32[]{:S(2)}) collective-permute-start(bf16[4,2,24,3072]{3,2,0,1:T(8,128)(2,1)} %dynamic-slice_bitcast_fusion.2), channel_id=1, source_target_pairs={{0,4},{1,5},{2,6},{3,7},{4,0},{5,1},{6,2},{7,3},{8,12},{9,13},{10,... | collective-permute-start | bytes 3538952 | tf_op jit(solution)/shard_map/ppermute | solution.py:36
  323.5 31.5 %collective-permute-start.41 = (bf16[4,2,96,768]{3,2,0,1:T(8,128)(2,1)}, bf16[4,2,96,768]{3,2,0,1:T(8,128)(2,1)}, u32[]{:S(2)}, u32[]{:S(2)}) collective-permute-start(bf16[4,2,96,768]{3,2,0,1:T(8,128)(2,1)} %dynamic-slice_bitcast_fusion.1), channel_id=1, source_target_pairs={{0,2},{1,3},{2,0},{3,1},{4,6},{5,7},{6,4},{7,5},{8,10},{9,11},{10,... | collective-permute-start | bytes 3538952 | tf_op jit(solution)/shard_map/ppermute | solution.py:36
  327.5 51.5 %collective-permute-start.29 = (bf16[4,2,24,3200]{3,2,1,0:T(8,128)(2,1)}, bf16[4,2,24,3200]{3,2,1,0:T(8,128)(2,1)}, u32[]{:S(2)}, u32[]{:S(2)}) collective-permute-start(bf16[4,2,24,3200]{3,2,1,0:T(8,128)(2,1)} %dynamic-slice_bitcast_fusion), channel_id=1, source_target_pairs={{0,2},{1,3},{2,0},{3,1},{4,6},{5,7},{6,4},{7,5},{8,10},{9,11},{10,... | collective-permute-start | bytes 3686408 | tf_op jit(solution)/shard_map/ppermute | solution.py:36
  339.8 42.0 %collective-permute-start.27 = (bf16[8,96,768]{2,1,0:T(8,128)(2,1)}, bf16[8,96,768]{2,1,0:T(8,128)(2,1)S(1)}, u32[]{:S(2)}, u32[]{:S(2)}) collective-permute-start(bf16[8,96,768]{2,1,0:T(8,128)(2,1)} %all-to-all-done.1), channel_id=1, source_target_pairs={{0,1},{1,0},{2,3},{3,2},{4,5},{5,4},{6,7},{7,6},{8,9},{9,8},{10,11... | collective-permute-start | bytes 3538952 | tf_op jit(solution)/shard_map/ppermute | solution.py:36
  354.4 49.4 %collective-permute-start.36 = (bf16[4,24,3072]{2,1,0:T(8,128)(2,1)}, bf16[4,24,3072]{2,1,0:T(8,128)(2,1)}, u32[]{:S(2)}, u32[]{:S(2)}) collective-permute-start(bf16[4,24,3072]{2,1,0:T(8,128)(2,1)} %dynamic-slice_bitcast_fusion.6), channel_id=1, source_target_pairs={{0,2},{1,3},{2,0},{3,1},{4,6},{5,7},{6,4},{7,5},{8,10},{9,11},{10,... | collective-permute-start | bytes 1769480 | tf_op jit(solution)/shard_map/ppermute | solution.py:36
  356.6 53.0 %collective-permute-start.42 = (bf16[4,96,768]{2,1,0:T(8,128)(2,1)S(1)}, bf16[4,96,768]{2,1,0:T(8,128)(2,1)}, u32[]{:S(2)}, u32[]{:S(2)}) collective-permute-start(bf16[4,96,768]{2,1,0:T(8,128)(2,1)S(1)} %dynamic-slice_bitcast_fusion.5), channel_id=1, source_target_pairs={{0,4},{1,5},{2,6},{3,7},{4,0},{5,1},{6,2},{7,3},{8,12},{9,13},{10,... | collective-permute-start | bytes 1769480 | tf_op jit(solution)/shard_map/ppermute | solution.py:36
  381.7 45.5 %collective-permute-start.30 = (bf16[4,24,3200]{2,1,0:T(8,128)(2,1)S(1)}, bf16[4,24,3200]{2,1,0:T(8,128)(2,1)S(1)}, u32[]{:S(2)}, u32[]{:S(2)}) collective-permute-start(bf16[4,24,3200]{2,1,0:T(8,128)(2,1)S(1)} %dynamic-slice_bitcast_fusion.4), channel_id=1, source_target_pairs={{0,4},{1,5},{2,6},{3,7},{4,0},{5,1},{6,2},{7,3},{8,12},{9,13},{10,... | collective-permute-start | bytes 1843208 | tf_op jit(solution)/shard_map/ppermute | solution.py:36
  405.2 8.4 %collective-permute-start.37 = (bf16[24,3072]{1,0:T(8,128)(2,1)S(1)}, bf16[24,3072]{1,0:T(8,128)(2,1)S(1)}, u32[]{:S(2)}, u32[]{:S(2)}) collective-permute-start(bf16[24,3072]{1,0:T(8,128)(2,1)S(1)} %get-tuple-element.137), channel_id=1, source_target_pairs={{0,8},{1,9},{2,10},{3,11},{4,12},{5,13},{6,14},{7,15},{8,0},{9,1},... | collective-permute-start | bytes 442376 | tf_op jit(solution)/shard_map/ppermute | solution.py:36
  407.0 11.6 %collective-permute-start.39 = (bf16[24,3072]{1,0:T(8,128)(2,1)S(1)}, bf16[24,3072]{1,0:T(8,128)(2,1)S(1)}, u32[]{:S(2)}, u32[]{:S(2)}) collective-permute-start(bf16[24,3072]{1,0:T(8,128)(2,1)S(1)} %get-tuple-element.138), channel_id=1, source_target_pairs={{0,24},{1,25},{2,26},{3,27},{4,28},{5,29},{6,30},{7,31},{8,16},{9,... | collective-permute-start | bytes 442376 | tf_op jit(solution)/shard_map/ppermute | solution.py:36
  409.6 16.8 %collective-permute-start.38 = (bf16[24,3072]{1,0:T(8,128)(2,1)S(1)}, bf16[24,3072]{1,0:T(8,128)(2,1)S(1)}, u32[]{:S(2)}, u32[]{:S(2)}) collective-permute-start(bf16[24,3072]{1,0:T(8,128)(2,1)S(1)} %get-tuple-element.139), channel_id=1, source_target_pairs={{0,16},{1,17},{2,18},{3,19},{4,20},{5,21},{6,22},{7,23},{8,24},{9,... | collective-permute-start | bytes 442376 | tf_op jit(solution)/shard_map/ppermute | solution.py:36
  410.9 24.5 %collective-permute-start.43 = (bf16[96,768]{1,0:T(8,128)(2,1)S(1)}, bf16[96,768]{1,0:T(8,128)(2,1)S(1)}, u32[]{:S(2)}, u32[]{:S(2)}) collective-permute-start(bf16[96,768]{1,0:T(8,128)(2,1)S(1)} %get-tuple-element.134), channel_id=1, source_target_pairs={{0,8},{1,9},{2,10},{3,11},{4,12},{5,13},{6,14},{7,15},{8,0},{9,1},... | collective-permute-start | bytes 442376 | tf_op jit(solution)/shard_map/ppermute | solution.py:36
  413.6 22.3 %collective-permute-start.45 = (bf16[96,768]{1,0:T(8,128)(2,1)S(1)}, bf16[96,768]{1,0:T(8,128)(2,1)S(1)}, u32[]{:S(2)}, u32[]{:S(2)}) collective-permute-start(bf16[96,768]{1,0:T(8,128)(2,1)S(1)} %get-tuple-element.135), channel_id=1, source_target_pairs={{0,24},{1,25},{2,26},{3,27},{4,28},{5,29},{6,30},{7,31},{8,16},{9,... | collective-permute-start | bytes 442376 | tf_op jit(solution)/shard_map/ppermute | solution.py:36
  418.6 19.3 %collective-permute-start.44 = (bf16[96,768]{1,0:T(8,128)(2,1)S(1)}, bf16[96,768]{1,0:T(8,128)(2,1)S(1)}, u32[]{:S(2)}, u32[]{:S(2)}) collective-permute-start(bf16[96,768]{1,0:T(8,128)(2,1)S(1)} %get-tuple-element.136), channel_id=1, source_target_pairs={{0,16},{1,17},{2,18},{3,19},{4,20},{5,21},{6,22},{7,23},{8,24},{9,... | collective-permute-start | bytes 442376 | tf_op jit(solution)/shard_map/ppermute | solution.py:36
  427.4 11.3 %collective-permute-start.31 = (bf16[24,3200]{1,0:T(8,128)(2,1)S(1)}, bf16[24,3200]{1,0:T(8,128)(2,1)S(1)}, u32[]{:S(2)}, u32[]{:S(2)}) collective-permute-start(bf16[24,3200]{1,0:T(8,128)(2,1)S(1)} %get-tuple-element.127), channel_id=1, source_target_pairs={{0,8},{1,9},{2,10},{3,11},{4,12},{5,13},{6,14},{7,15},{8,0},{9,1},... | collective-permute-start | bytes 460808 | tf_op jit(solution)/shard_map/ppermute | solution.py:36
  432.4 7.9 %collective-permute-start.33 = (bf16[24,3200]{1,0:T(8,128)(2,1)S(1)}, bf16[24,3200]{1,0:T(8,128)(2,1)S(1)}, u32[]{:S(2)}, u32[]{:S(2)}) collective-permute-start(bf16[24,3200]{1,0:T(8,128)(2,1)S(1)} %get-tuple-element.128), channel_id=1, source_target_pairs={{0,24},{1,25},{2,26},{3,27},{4,28},{5,29},{6,30},{7,31},{8,16},{9,... | collective-permute-start | bytes 460808 | tf_op jit(solution)/shard_map/ppermute | solution.py:36
  435.4 10.7 %collective-permute-start.32 = (bf16[24,3200]{1,0:T(8,128)(2,1)S(1)}, bf16[24,3200]{1,0:T(8,128)(2,1)S(1)}, u32[]{:S(2)}, u32[]{:S(2)}) collective-permute-start(bf16[24,3200]{1,0:T(8,128)(2,1)S(1)} %get-tuple-element.129), channel_id=1, source_target_pairs={{0,16},{1,17},{2,18},{3,19},{4,20},{5,21},{6,22},{7,23},{8,24},{9,... | collective-permute-start | bytes 460808 | tf_op jit(solution)/shard_map/ppermute | solution.py:36
  (85 other events, 483.3 us)
